TPU v7x, 32 devices: a whole 2x2x4 slice. The times are simulated.
32 devices in a mesh: rep: 8 (over y, x, core), fsdp: 4 (over z).
Axes of the slice: x: 2, y: 2, z: 4, core: 2. Of those that a mesh axis runs over, the one named last changes fastest.
Arguments:
- latents: float32 [2, 32, 320, 256], P(None, ('rep', 'fsdp')), may hold values from -6 to 6
- gaussian: float32 [2, 32, 320, 256], P(None, ('rep', 'fsdp')), may hold values from -6 to 6
- stamps: int32 [2, 32], P(None, ('rep', 'fsdp')), may hold values from 0 to 999
- numerator: float32 [8, 320, 2880], P('rep', 'fsdp'), may hold values from -6 to 6
- momentum: float32 [8, 320, 2880], P('rep', 'fsdp'), may hold values from -1.5 to 1.5
- push_weight: float32 [8], P('rep'), may hold values from 0.5 to 2
- arrived_numerator: float32 [8, 320, 2880], P('rep', 'fsdp'), may hold values from -6 to 6
- arrived_weight: float32 [8], P('rep'), may hold values from 0.25 to 1
Outputs:
- numerator_out: float32 [8, 320, 2880], P('rep', 'fsdp')
- momentum_out: float32 [8, 320, 2880], P('rep', 'fsdp')
- weight_out: float32 [8], P('rep')
- pending_numerator: float32 [8, 320, 2880], P('rep', 'fsdp')
- pending_weight: float32 [8], P('rep')
All inputs are finite; a program needn't handle non-finite values.
Results may differ from a plain program's by a relative error of at most 0.0003.
Values sent between devices are 32-bit elements; how exact they have to be, the bound alone decides.
A program may use at most 64 MiB of HBM per device.

v0:
```python
import functools

import jax
import jax.numpy as jnp
from jax import lax
from jax.experimental import pallas as pl
from jax.experimental.pallas import tpu as pltpu
from jax.sharding import PartitionSpec as P

GROUPS = 32
CROP_H = 16
CROP_W = 16
STEPS = 2
TRAIN_T = 1000
TAPS = 9

norm_epsilon = 1e-05
momentum_decay = 0.9
step_size = 1.0
beta_first = 0.00085
beta_last = 0.012
MESH = pl.DeviceIdType.MESH


def split(value):
    high = value.astype(jnp.bfloat16)
    return high, (value - high.astype(jnp.float32)).astype(jnp.bfloat16)


def product(a, b, contract):
    dims = ((contract[0], contract[1]), ((), ()))
    dot = functools.partial(
        lax.dot_general, dimension_numbers=dims, preferred_element_type=jnp.float32
    )
    return dot(a[0], b[0]) + (dot(a[0], b[1]) + dot(a[1], b[0]))


def noise_level(stamp):
    rows = -(-TRAIN_T // 128)
    shape = (rows, 128)
    position = lax.broadcasted_iota(jnp.int32, shape, 0) * 128 + lax.broadcasted_iota(
        jnp.int32, shape, 1
    )
    fraction = position.astype(jnp.float32) / (TRAIN_T - 1)
    root_first = beta_first**0.5
    root_last = beta_last**0.5
    root = root_first + fraction * (root_last - root_first)
    factor = jnp.where(position <= stamp, 1.0 - root * root, jnp.float32(1.0))
    for shift in (64, 32, 16, 8, 4, 2, 1):
        factor = factor * pltpu.roll(factor, shift, 1)
    for shift in (4, 2, 1):
        factor = factor * pltpu.roll(factor, shift, 0)
    return factor


def group_mean(value, same_group, count):
    row = jnp.sum(value, axis=1, keepdims=True)
    row = jnp.broadcast_to(row, (row.shape[0], 128))
    first = row.astype(jnp.bfloat16)
    rest = row - first.astype(jnp.float32)
    second = rest.astype(jnp.bfloat16)
    third = (rest - second.astype(jnp.float32)).astype(jnp.bfloat16)
    dot = functools.partial(jnp.dot, preferred_element_type=jnp.float32)
    total = dot(same_group, first) + (dot(same_group, second) + dot(same_group, third))
    return total[:, 0:1] * (1.0 / count)


def tap_shift(tap):
    return (tap // 3 - 1) * CROP_W + (tap % 3 - 1)


def tap_mask(tap, pixels):
    place = lax.broadcasted_iota(jnp.int32, (1, pixels), 1)
    row = place // CROP_W + (tap // 3 - 1)
    col = place % CROP_W + (tap % 3 - 1)
    return (row >= 0) & (row < CROP_H) & (col >= 0) & (col < CROP_W)


def body(
    sizes,
    stamps, weight, arrived_weight,
    latents_in, gaussian_in, numerator_in, momentum_in, arrived_in,
    numerator_out, momentum_out, weight_out, pending_out, pending_weight_out,
    latents, gaussian, numerator, momentum, arrived, fetch_sem,
    acts, gap_own, gap_rows, kernel_hi, kernel_lo, res_hi, res_lo, total, taps_out,
    outbox, inbox, weight_box,
    acts_send, acts_recv, gap_send, gap_recv, push_send, push_recv, weight_send, weight_recv,
):
    reps, shards, padded, chunk = sizes
    rows, columns = numerator.shape
    channels, pixels = latents.shape[1:]
    replica_batch = shards
    tap_scale = columns ** (-0.5)
    rep = lax.axis_index("rep")
    me = lax.axis_index("fsdp")

    def fetch(index, source, target):
        return pltpu.make_async_copy(source, target, fetch_sem.at[index])

    samples_in = [
        (
            fetch(2 * step, latents_in.at[step], latents.at[step]),
            fetch(2 * step + 1, gaussian_in.at[step], gaussian.at[step]),
        )
        for step in range(STEPS)
    ]
    state_in = [
        fetch(2 * STEPS, numerator_in, numerator),
        fetch(2 * STEPS + 1, momentum_in, momentum),
        fetch(2 * STEPS + 2, arrived_in, arrived),
    ]
    for pair in samples_in:
        for copy in pair:
            copy.start()
    for copy in state_in:
        copy.start()

    offsets = sorted({2**k % reps for k in range(STEPS)} | {-(2**k) % reps for k in range(STEPS)})
    barrier = pltpu.get_barrier_semaphore()
    for offset in range(1, shards):
        pl.semaphore_signal(
            barrier, inc=1, device_id={"fsdp": lax.rem(me + offset, shards)}, device_id_type=MESH
        )
    for offset in offsets:
        pl.semaphore_signal(
            barrier, inc=1, device_id={"rep": lax.rem(rep + offset, reps)}, device_id_type=MESH
        )

    def acts_copy(step, owner, right):
        side = 1 if right else 0
        return pltpu.make_async_remote_copy(
            src_ref=acts.at[step, owner],
            dst_ref=acts.at[step, owner],
            send_sem=acts_send.at[side, step, owner],
            recv_sem=acts_recv.at[step, owner],
            device_id={"fsdp": me + 1 if right else me - 1},
            device_id_type=MESH,
        )

    def gap_copy(step, target):
        return pltpu.make_async_remote_copy(
            src_ref=gap_own.at[step, target],
            dst_ref=gap_rows.at[step, me],
            send_sem=gap_send.at[step, target],
            recv_sem=gap_recv.at[step, me],
            device_id={"fsdp": target},
            device_id_type=MESH,
        )

    def gap_arrival(step, owner):
        return pltpu.make_async_remote_copy(
            src_ref=gap_own.at[step, owner],
            dst_ref=gap_rows.at[step, owner],
            send_sem=gap_send.at[step, owner],
            recv_sem=gap_recv.at[step, owner],
            device_id={"fsdp": owner},
            device_id_type=MESH,
        )

    def push_copy(step, part):
        span = pl.ds(part * chunk, chunk)
        target = (inbox if step < STEPS - 1 else pending_out).at[span]
        return pltpu.make_async_remote_copy(
            src_ref=outbox.at[step, span],
            dst_ref=target,
            send_sem=push_send.at[step, part],
            recv_sem=push_recv.at[step, part],
            device_id={"rep": lax.rem(rep + 2**step, reps)},
            device_id_type=MESH,
        )

    def weight_copy(step):
        return pltpu.make_async_remote_copy(
            src_ref=weight_box.at[0, step],
            dst_ref=weight_box.at[1, step],
            send_sem=weight_send.at[step],
            recv_sem=weight_recv.at[step],
            device_id={"rep": lax.rem(rep + 2**step, reps)},
            device_id_type=MESH,
        )

    def send_own(step, right):
        @pl.when(me < shards - 1 if right else me > 0)
        def _():
            acts_copy(step, me, right).start()
            for away in range(1, shards):
                target = me + away if right else me - away

                @pl.when(target < shards if right else target >= 0)
                def _():
                    gap_copy(step, target).start()

    same_group = (
        lax.broadcasted_iota(jnp.int32, (channels, channels), 0) // (channels // GROUPS)
        == lax.broadcasted_iota(jnp.int32, (channels, channels), 1) // (channels // GROUPS)
    ).astype(jnp.float32).astype(jnp.bfloat16)
    count = (channels // GROUPS) * pixels

    def activate(step):
        level = noise_level(stamps[step])[0:1, 0:1]
        for copy in samples_in[step]:
            copy.wait()
        noise = gaussian[step]
        noised = jnp.sqrt(level) * latents[step] + jnp.sqrt(1.0 - level) * noise
        gap = noised - noise
        for target in range(shards):
            gap_own[step, target] = gap[target * rows : (target + 1) * rows]
        centered = noised - group_mean(noised, same_group, count)
        spread = group_mean(centered * centered, same_group, count)
        normed = centered * lax.rsqrt(spread + norm_epsilon)
        acts[step, me] = normed / (1.0 + jnp.exp(-normed))
        gap_rows[step, me] = gap_own[step, me]

    activate(0)
    first_weight = jnp.broadcast_to(weight[...], weight_box.shape[2:])
    weight_box[0, 0] = 0.5 * first_weight
    second_weight = 0.5 * first_weight + jnp.broadcast_to(
        arrived_weight[...], weight_box.shape[2:]
    )
    weight_box[0, 1] = 0.5 * second_weight
    pl.semaphore_wait(barrier, shards - 1 + len(offsets))
    send_own(0, True)
    send_own(0, False)
    for step in range(STEPS):
        weight_copy(step).start()
    for step in range(1, STEPS):
        activate(step)

    @pl.when(me == 0)
    def _():
        for step in range(1, STEPS):
            send_own(step, True)

    @pl.when(me == shards - 1)
    def _():
        for step in range(1, STEPS):
            send_own(step, False)

    if padded != rows:
        for ref in (kernel_hi, kernel_lo, res_hi, res_lo):
            ref[...] = jnp.zeros(ref.shape, ref.dtype)

    def set_kernel(tap, first, values):
        high, low = split(values)
        start = tap * padded + first
        kernel_hi[start : start + values.shape[0]] = high
        kernel_lo[start : start + values.shape[0]] = low

    for copy in state_in:
        copy.wait()
    for tap in range(TAPS):
        set_kernel(
            tap, 0, numerator[:, tap * channels : (tap + 1) * channels] / first_weight[0:1, 0:1]
        )

    def process(step, owner):
        signal = split(acts[step, owner])
        taps_out[...] = product((kernel_hi[...], kernel_lo[...]), signal, ((1,), (0,)))
        output = jnp.zeros((rows, pixels), jnp.float32)
        for tap in range(TAPS):
            value = taps_out[tap * padded : tap * padded + rows]
            moved = pltpu.roll(value, -tap_shift(tap) % pixels, 1) if tap_shift(tap) else value
            output += jnp.where(tap_mask(tap, pixels), moved, 0.0)
        residual = gap_rows[step, owner] + tap_scale * output
        for tap in range(TAPS):
            value = jnp.where(tap_mask(tap, pixels), residual, 0.0)
            if tap_shift(tap):
                value = pltpu.roll(value, tap_shift(tap) % pixels, 1)
            high, low = split(value)
            res_hi[tap * padded : tap * padded + rows] = high
            res_lo[tap * padded : tap * padded + rows] = low
        total[...] += product((res_hi[...], res_lo[...]), signal, ((1,), (1,)))

    for step in range(STEPS):
        total[...] = jnp.zeros(total.shape, jnp.float32)

        def visit(k, _, step=step):
            away = (k + 1) // 2
            owner = jnp.where(lax.rem(k, 2) == 1, me - away, me + away)

            @pl.when((owner >= 0) & (owner < shards))
            def _():
                @pl.when(owner < me)
                def _():
                    acts_copy(step, owner, True).wait_recv()

                    @pl.when(me < shards - 1)
                    def _():
                        acts_copy(step, owner, True).start()

                    if step < STEPS - 1:

                        @pl.when(owner == 0)
                        def _():
                            send_own(step + 1, True)

                @pl.when(owner > me)
                def _():
                    acts_copy(step, owner, False).wait_recv()

                    @pl.when(me > 0)
                    def _():
                        acts_copy(step, owner, False).start()

                    if step < STEPS - 1:

                        @pl.when(owner == shards - 1)
                        def _():
                            send_own(step + 1, False)

                @pl.when(owner != me)
                def _():
                    gap_arrival(step, owner).wait_recv()

                process(step, owner)

            return 0

        lax.fori_loop(0, 2 * shards - 1, visit, 0)

        if step > 0:
            for part in range(rows // chunk):
                push_copy(step - 1, part).wait_recv()
        for part in range(rows // chunk):
            span = slice(part * chunk, (part + 1) * chunk)
            for tap in range(TAPS):
                cut = slice(tap * channels, (tap + 1) * channels)
                start = tap * padded + part * chunk
                gradient = total[start : start + chunk] * (tap_scale / replica_batch)
                old = (momentum if step == 0 else momentum_out)[span, cut]
                new = momentum_decay * old + gradient
                momentum_out[span, cut] = new
                base = (numerator if step == 0 else numerator_out)[span, cut]
                half = 0.5 * (base - step_size * new)
                outbox[step, span, cut] = half
                fresh = half + (arrived if step == 0 else inbox)[span, cut]
                numerator_out[span, cut] = fresh
                if step < STEPS - 1:
                    set_kernel(tap, part * chunk, fresh / second_weight[0:1, 0:1])
            push_copy(step, part).start()

    for step in range(STEPS):
        weight_copy(step).wait_recv()
    weight_out[...] = (0.5 * second_weight + weight_box[1, 0])[0:1, 0:1]
    pending_weight_out[...] = weight_box[1, 1][0:1, 0:1]
    for step in range(STEPS):
        weight_copy(step).wait_send()
        for part in range(rows // chunk):
            push_copy(step, part).wait_send()
            if step == STEPS - 1:
                push_copy(step, part).wait_recv()

        def drain(owner, _, step=step):
            @pl.when((owner <= me) & (me < shards - 1))
            def _():
                acts_copy(step, owner, True).wait_send()

            @pl.when((owner >= me) & (me > 0))
            def _():
                acts_copy(step, owner, False).wait_send()

            @pl.when(owner != me)
            def _():
                gap_copy(step, owner).wait_send()

            return 0

        lax.fori_loop(0, shards, drain, 0)


def deliver(first_in, second_in, third_in, first_out, second_out, third_out, sems):
    pairs = ((first_in, first_out), (second_in, second_out), (third_in, third_out))
    copies = [
        pltpu.make_async_copy(source, target, sems.at[k])
        for k, (source, target) in enumerate(pairs)
    ]
    for copy in copies:
        copy.start()
    for copy in copies:
        copy.wait()


def solution(mesh):
    reps, shards = mesh.shape["rep"], mesh.shape["fsdp"]

    def local(
        latents, gaussian, stamps, numerator, momentum, push_weight, arrived, arrived_weight
    ):
        steps, samples, channels, pixels = latents.shape
        rows, columns = numerator.shape[1:]
        assert samples == 1 and steps == STEPS
        padded = -(-rows // 16) * 16
        chunk = 16 if rows % 16 == 0 else rows
        parts = rows // chunk
        vmem = pl.BlockSpec(memory_space=pltpu.VMEM)
        dma = pltpu.SemaphoreType.DMA
        state = pltpu.VMEM((rows, columns), jnp.float32)
        one = jax.ShapeDtypeStruct((1, 1), jnp.float32)
        outs = pl.pallas_call(
            functools.partial(body, (reps, shards, padded, chunk)),
            out_shape=(state, state, one, state, one),
            in_specs=[pl.BlockSpec(memory_space=pltpu.SMEM), vmem, vmem]
            + [pl.BlockSpec(memory_space=pl.ANY)] * 5,
            out_specs=(vmem,) * 5,
            scratch_shapes=[
                pltpu.VMEM((steps, channels, pixels), jnp.float32),
                pltpu.VMEM((steps, channels, pixels), jnp.float32),
                pltpu.VMEM((rows, columns), jnp.float32),
                pltpu.VMEM((rows, columns), jnp.float32),
                pltpu.VMEM((rows, columns), jnp.float32),
                dma((2 * steps + 3,)),
                pltpu.VMEM((steps, shards, channels, pixels), jnp.float32),
                pltpu.VMEM((steps, shards, rows, pixels), jnp.float32),
                pltpu.VMEM((steps, shards, rows, pixels), jnp.float32),
                pltpu.VMEM((TAPS * padded, channels), jnp.bfloat16),
                pltpu.VMEM((TAPS * padded, channels), jnp.bfloat16),
                pltpu.VMEM((TAPS * padded, pixels), jnp.bfloat16),
                pltpu.VMEM((TAPS * padded, pixels), jnp.bfloat16),
                pltpu.VMEM((TAPS * padded, channels), jnp.float32),
                pltpu.VMEM((TAPS * padded, pixels), jnp.float32),
                pltpu.VMEM((steps, rows, columns), jnp.float32),
                pltpu.VMEM((rows, columns), jnp.float32),
                pltpu.VMEM((2, steps, 8, 128), jnp.float32),
                dma((2, steps, shards)),
                dma((steps, shards)),
                dma((steps, shards)),
                dma((steps, shards)),
                dma((steps, parts)),
                dma((steps, parts)),
                dma((steps,)),
                dma((steps,)),
            ],
            compiler_params=pltpu.CompilerParams(
                collective_id=0, has_side_effects=True, vmem_limit_bytes=56 * 1024 * 1024
            ),
        )(
            stamps.reshape(steps),
            push_weight.reshape(1, 1),
            arrived_weight.reshape(1, 1),
            latents.reshape(steps, channels, pixels),
            gaussian.reshape(steps, channels, pixels),
            numerator[0],
            momentum[0],
            arrived[0],
        )
        stored = jax.ShapeDtypeStruct((rows, columns), jnp.float32)
        results = pl.pallas_call(
            deliver,
            out_shape=(stored,) * 3,
            in_specs=[vmem] * 3,
            out_specs=(pl.BlockSpec(memory_space=pl.ANY),) * 3,
            scratch_shapes=[dma((3,))],
            compiler_params=pltpu.CompilerParams(vmem_limit_bytes=48 * 1024 * 1024),
        )(outs[0], outs[1], outs[3])
        return (results[0][None], results[1][None], outs[2][0], results[2][None], outs[4][0])

    in_specs = (
        P(None, ("rep", "fsdp"), None, None),
        P(None, ("rep", "fsdp"), None, None),
        P(None, ("rep", "fsdp")),
        P("rep", "fsdp", None),
        P("rep", "fsdp", None),
        P("rep"),
        P("rep", "fsdp", None),
        P("rep"),
    )
    out_specs = (
        P("rep", "fsdp", None),
        P("rep", "fsdp", None),
        P("rep"),
        P("rep", "fsdp", None),
        P("rep"),
    )
    return jax.shard_map(local, mesh=mesh, in_specs=in_specs, out_specs=out_specs, check_vma=False)
```

profile of v0, /device:TPU:0, one launch (start us, length us, event | category | flops | bytes accessed | tf_op | source)
XLA Modules:
  0.0 91.5 jit_solution(7518325016981176399)
XLA Ops:
  1.9 84.5 %shard_map.119 = (f32[80,2880]{1,0:T(8,128)S(1)}, f32[80,2880]{1,0:T(8,128)S(1)}, f32[1,1]{1,0:T(1,128)}, f32[80,2880]{1,0:T(8,128)S(1)}, f32[1,1]{1,0:T(1,128)}) custom-call(s32[2]{0:T(128)} %bitcast.20, f32[1,1]{1,0:T(1,128)} %bitcast.13.weight, f32[1,1]{1,0:T(1,128)} %bitcast.14.arrived_weight, f32[2,320,256]{2,1,0:T(8,128)} %bitcast.18, ...), custom_call_target="tpu_custom_call" | custom-call | tf_op jit(solution)/shard_map/pallas_call | solution.py:399
  86.4 1.6 %shard_map.120 = (f32[80,2880]{1,0:T(8,128)}, f32[80,2880]{1,0:T(8,128)}, f32[80,2880]{1,0:T(8,128)}) custom-call(f32[80,2880]{1,0:T(8,128)S(1)} %get-tuple-element.13.first_in, f32[80,2880]{1,0:T(8,128)S(1)} %get-tuple-element.14.second_in, f32[80,2880]{1,0:T(8,128)S(1)} %get-tuple-element.15.third_in), custom_call_target="tpu_custom_call" | custom-call | tf_op jit(solution)/shard_map/pallas_call | solution.py:447
where the time goes:
time: 91.7 us; the launch traced here: 91.5 us
  Pallas kernels  86 us (94%)
  between operations  5.46 us (6%)
    pallas_call x1, Pallas kernels, local(): pl.pallas_call(functools.partial(body, (reps, shards, padded, chunk)), ou...  84.5 us

commit v1 on v0

--- a/solution.py
+++ b/solution.py
@@ -83,7 +83,7 @@
     numerator_out, momentum_out, weight_out, pending_out, pending_weight_out,
     latents, gaussian, numerator, momentum, arrived, fetch_sem,
     acts, gap_own, gap_rows, kernel_hi, kernel_lo, res_hi, res_lo, total, taps_out,
-    outbox, inbox, weight_box,
+    outbox, inbox, weight_box, relay_box, relay_sem,
     acts_send, acts_recv, gap_send, gap_recv, push_send, push_recv, weight_send, weight_recv,
 ):
     reps, shards, padded, chunk = sizes
@@ -124,6 +124,53 @@
     for offset in offsets:
         pl.semaphore_signal(
             barrier, inc=1, device_id={"rep": lax.rem(rep + offset, reps)}, device_id_type=MESH
+        )
+
+    detour = shards >= 4
+    last_part = rows // chunk - 1
+    at_end = (me == 0) | (me == shards - 1)
+    beside_end = (me == 1) | (me == shards - 2)
+    end = jnp.where(me <= 1, 0, shards - 1)
+    beside = jnp.where(me <= 1, 1, shards - 2)
+    last_shift = 2 ** (STEPS - 1)
+    if detour:
+
+        @pl.when(at_end)
+        def _():
+            pl.semaphore_signal(
+                barrier,
+                inc=1,
+                device_id={"rep": lax.rem(rep + last_shift, reps), "fsdp": beside},
+                device_id_type=MESH,
+            )
+
+        @pl.when(beside_end)
+        def _():
+            pl.semaphore_signal(
+                barrier,
+                inc=1,
+                device_id={"rep": lax.rem(rep + reps - last_shift % reps, reps), "fsdp": end},
+                device_id_type=MESH,
+            )
+
+    def to_relay():
+        return pltpu.make_async_remote_copy(
+            src_ref=outbox.at[STEPS - 1, pl.ds(last_part * chunk, chunk)],
+            dst_ref=relay_box,
+            send_sem=relay_sem.at[0],
+            recv_sem=relay_sem.at[1],
+            device_id={"rep": lax.rem(rep + last_shift, reps), "fsdp": beside},
+            device_id_type=MESH,
+        )
+
+    def from_relay():
+        return pltpu.make_async_remote_copy(
+            src_ref=relay_box,
+            dst_ref=pending_out.at[pl.ds(last_part * chunk, chunk)],
+            send_sem=relay_sem.at[2],
+            recv_sem=push_recv.at[STEPS - 1, last_part],
+            device_id={"fsdp": end},
+            device_id_type=MESH,
         )
 
     def acts_copy(step, owner, right):
@@ -218,7 +265,10 @@
         arrived_weight[...], weight_box.shape[2:]
     )
     weight_box[0, 1] = 0.5 * second_weight
-    pl.semaphore_wait(barrier, shards - 1 + len(offsets))
+    peers = shards - 1 + len(offsets)
+    if detour:
+        peers = peers + jnp.where(at_end | beside_end, 1, 0)
+    pl.semaphore_wait(barrier, peers)
     send_own(0, True)
     send_own(0, False)
     for step in range(STEPS):
@@ -321,7 +371,8 @@
         if step > 0:
             for part in range(rows // chunk):
                 push_copy(step - 1, part).wait_recv()
-        for part in range(rows // chunk):
+        order = list(range(rows // chunk))
+        for part in order[-1:] + order[:-1]:
             span = slice(part * chunk, (part + 1) * chunk)
             for tap in range(TAPS):
                 cut = slice(tap * channels, (tap + 1) * channels)
@@ -337,7 +388,25 @@
                 numerator_out[span, cut] = fresh
                 if step < STEPS - 1:
                     set_kernel(tap, part * chunk, fresh / second_weight[0:1, 0:1])
-            push_copy(step, part).start()
+            if detour and step == STEPS - 1 and part == last_part:
+
+                @pl.when(at_end)
+                def _():
+                    to_relay().start()
+
+                @pl.when(jnp.logical_not(at_end))
+                def _():
+                    push_copy(STEPS - 1, last_part).start()
+
+            else:
+                push_copy(step, part).start()
+
+    if detour:
+
+        @pl.when(beside_end)
+        def _():
+            to_relay().wait_recv()
+            from_relay().start()
 
     for step in range(STEPS):
         weight_copy(step).wait_recv()
@@ -346,7 +415,22 @@
     for step in range(STEPS):
         weight_copy(step).wait_send()
         for part in range(rows // chunk):
-            push_copy(step, part).wait_send()
+            if detour and step == STEPS - 1 and part == last_part:
+
+                @pl.when(at_end)
+                def _():
+                    to_relay().wait_send()
+
+                @pl.when(jnp.logical_not(at_end))
+                def _():
+                    push_copy(STEPS - 1, last_part).wait_send()
+
+                @pl.when(beside_end)
+                def _():
+                    from_relay().wait_send()
+
+            else:
+                push_copy(step, part).wait_send()
             if step == STEPS - 1:
                 push_copy(step, part).wait_recv()
 
@@ -421,6 +505,8 @@
                 pltpu.VMEM((steps, rows, columns), jnp.float32),
                 pltpu.VMEM((rows, columns), jnp.float32),
                 pltpu.VMEM((2, steps, 8, 128), jnp.float32),
+                pltpu.VMEM((chunk, columns), jnp.float32),
+                dma((3,)),
                 dma((2, steps, shards)),
                 dma((steps, shards)),
                 dma((steps, shards)),

time: 91.7 us -> 87.8 us (0.957)
  Pallas kernels: 86 us -> 82.1 us
    pallas_call x1, Pallas kernels: 84.5 us -> 80.6 us  [local(): pl.pallas_call(functools.partial(body, (reps, shards, padded, chunk)), ou...]
where the time goes in v1:
time: 87.8 us; the launch traced here: 87.6 us
  Pallas kernels  82.1 us (94%)
  between operations  5.46 us (6%)
    pallas_call x1, Pallas kernels, local(): pl.pallas_call(functools.partial(body, (reps, shards, padded, chunk)), ou...  80.6 us

profile of v1, /device:TPU:0, one launch (start us, length us, event | category | flops | bytes accessed | tf_op | source)
XLA Modules:
  0.0 87.6 jit_solution(16414955502392789985)
XLA Ops:
  1.9 80.6 %shard_map.119 = (f32[80,2880]{1,0:T(8,128)S(1)}, f32[80,2880]{1,0:T(8,128)S(1)}, f32[1,1]{1,0:T(1,128)}, f32[80,2880]{1,0:T(8,128)S(1)}, f32[1,1]{1,0:T(1,128)}) custom-call(s32[2]{0:T(128)} %bitcast.20, f32[1,1]{1,0:T(1,128)} %bitcast.13.weight, f32[1,1]{1,0:T(1,128)} %bitcast.14.arrived_weight, f32[2,320,256]{2,1,0:T(8,128)} %bitcast.18, ...), custom_call_target="tpu_custom_call" | custom-call | tf_op jit(solution)/shard_map/pallas_call | solution.py:483
  82.5 1.6 %shard_map.120 = (f32[80,2880]{1,0:T(8,128)}, f32[80,2880]{1,0:T(8,128)}, f32[80,2880]{1,0:T(8,128)}) custom-call(f32[80,2880]{1,0:T(8,128)S(1)} %get-tuple-element.13.first_in, f32[80,2880]{1,0:T(8,128)S(1)} %get-tuple-element.14.second_in, f32[80,2880]{1,0:T(8,128)S(1)} %get-tuple-element.15.third_in), custom_call_target="tpu_custom_call" | custom-call | tf_op jit(solution)/shard_map/pallas_call | solution.py:533

commit v2 on v1

--- a/solution.py
+++ b/solution.py
@@ -238,8 +238,8 @@
                     gap_copy(step, target).start()
 
     same_group = (
-        lax.broadcasted_iota(jnp.int32, (channels, channels), 0) // (channels // GROUPS)
-        == lax.broadcasted_iota(jnp.int32, (channels, channels), 1) // (channels // GROUPS)
+        lax.broadcasted_iota(jnp.int32, (channels, 1), 0) // (channels // GROUPS)
+        == lax.broadcasted_iota(jnp.int32, (1, channels), 1) // (channels // GROUPS)
     ).astype(jnp.float32).astype(jnp.bfloat16)
     count = (channels // GROUPS) * pixels
 

time: 87.8 us -> 87.8 us (level)
  no operation moved by 1% of the time
where the time goes in v2:
time: 87.8 us; the launch traced here: 87.6 us
  Pallas kernels  82.1 us (94%)
  between operations  5.46 us (6%)
    pallas_call x1, Pallas kernels, local(): pl.pallas_call(functools.partial(body, (reps, shards, padded, chunk)), ou...  80.6 us

profile of v2, /device:TPU:0, one launch (start us, length us, event | category | flops | bytes accessed | tf_op | source)
XLA Modules:
  0.0 87.6 jit_solution(16414955502392789985)
XLA Ops:
  1.9 80.6 %shard_map.119 = (f32[80,2880]{1,0:T(8,128)S(1)}, f32[80,2880]{1,0:T(8,128)S(1)}, f32[1,1]{1,0:T(1,128)}, f32[80,2880]{1,0:T(8,128)S(1)}, f32[1,1]{1,0:T(1,128)}) custom-call(s32[2]{0:T(128)} %bitcast.20, f32[1,1]{1,0:T(1,128)} %bitcast.13.weight, f32[1,1]{1,0:T(1,128)} %bitcast.14.arrived_weight, f32[2,320,256]{2,1,0:T(8,128)} %bitcast.18, ...), custom_call_target="tpu_custom_call" | custom-call | tf_op jit(solution)/shard_map/pallas_call | solution.py:483
  82.5 1.6 %shard_map.120 = (f32[80,2880]{1,0:T(8,128)}, f32[80,2880]{1,0:T(8,128)}, f32[80,2880]{1,0:T(8,128)}) custom-call(f32[80,2880]{1,0:T(8,128)S(1)} %get-tuple-element.13.first_in, f32[80,2880]{1,0:T(8,128)S(1)} %get-tuple-element.14.second_in, f32[80,2880]{1,0:T(8,128)S(1)} %get-tuple-element.15.third_in), custom_call_target="tpu_custom_call" | custom-call | tf_op jit(solution)/shard_map/pallas_call | solution.py:533
